TPU v7x, 32 devices: a whole 2x2x4 slice. The times are simulated.
32 devices in a mesh: seq: 8 (over z, y), tp: 4 (over x, core).
Axes of the slice: x: 2, y: 2, z: 4, core: 2. Of those that a mesh axis runs over, the one named last changes fastest.
Arguments:
- tokens: bfloat16 [8192, 1152], P('seq', 'tp'), may hold values from -6 to 6
- out_grad: bfloat16 [8192, 1152], P('seq', 'tp'), may hold values from -6 to 6
- route_mask: int32 [8192], P('seq'), may hold values from 0 to 1, as said below
- kept_counts: int32 [32], replicated, may hold values from 64 to 192, as said below
- labels: int32 [32], replicated, may hold values from 0 to 1000
- timesteps: int32 [32], replicated, may hold values from 0 to 999
- class_table: bfloat16 [1001, 1152], replicated, may hold values from -6 to 6
- ada_weight: bfloat16 [1152, 6, 1152], P(None, None, 'tp'), may hold values from -0.1875 to 0.1875
- ada_bias: bfloat16 [6, 1152], P(None, 'tp'), may hold values from -2 to 2
- qkv_weight: bfloat16 [1152, 3, 1152], P(None, None, 'tp'), may hold values from -0.1875 to 0.1875
- qv_bias: bfloat16 [2, 1152], P(None, 'tp'), may hold values from -2 to 2
- proj_weight: bfloat16 [1152, 1152], P('tp'), may hold values from -0.5 to 0.5
- proj_bias: bfloat16 [1152], P('tp'), may hold values from -2 to 2
- hidden_weight: bfloat16 [1152, 4608], P(None, 'tp'), may hold values from -0.1875 to 0.1875
- hidden_bias: bfloat16 [4608], P('tp'), may hold values from -2 to 2
- output_weight: bfloat16 [4608, 1152], P('tp'), may hold values from -0.09375 to 0.09375
- output_bias: bfloat16 [1152], P('tp'), may hold values from -2 to 2
Outputs:
- output: bfloat16 [8192, 1152], P('seq', 'tp')
- tokens_grad: bfloat16 [8192, 1152], P('seq', 'tp')
- class_grad: float32 [1001, 1152], P(None, 'seq')
- ada_weight_grad: float32 [1152, 6, 1152], P('seq', None, 'tp')
- ada_bias_grad: float32 [6, 1152], P(None, 'tp')
- qkv_weight_grad: float32 [1152, 3, 1152], P('seq', None, 'tp')
- qv_bias_grad: float32 [2, 1152], P(None, 'tp')
- proj_weight_grad: float32 [1152, 1152], P('tp', 'seq')
- proj_bias_grad: float32 [1152], P('tp')
- hidden_weight_grad: float32 [1152, 4608], P('seq', 'tp')
- hidden_bias_grad: float32 [4608], P('tp')
- output_weight_grad: float32 [4608, 1152], P('tp', 'seq')
- output_bias_grad: float32 [1152], P('tp')
Inputs may be any that keep to these rules, and one draw needn't show every extreme that they name: route_mask keeps exactly kept_counts[i] of the 256 tokens of image i. The kept tokens of all images number 512 * 8; the kept tokens of the first j * 4 images exceed j * 512 by 0 to 128 for every j, by exactly 128 for some j, and by 0 at the end. Every aligned block of 4 images has one image with 192 kept tokens. `route_mask`: consistent with kept_counts.
All inputs are finite; a program needn't handle non-finite values.
Results may differ from a plain program's by a relative error of at most 0.025.
The roundings to bfloat16 on the way count: a program that leaves them out, or rounds other values in their place, can miss the bound.
Values may be sent and summed in bfloat16 or wider, within the bound.
A program may use at most 192 MiB of HBM per device.

v0:
```python
import math
import jax
import jax.numpy as jnp
from jax import lax
from jax.sharding import PartitionSpec as P

HEAD_DIM = 72
IMG_DEV = 4
KEEP_MOST = 192
K_ROWS = 512
SPILL = 128
NORM_EPS = 1e-06
HIGHEST = lax.Precision.HIGHEST


def passed_along(array, axis, by):
    devices = lax.axis_size(axis)
    pairs = [(i, i + by) for i in range(devices) if 0 <= i + by < devices]
    return lax.ppermute(array, axis, pairs)


def padded(array, sides, width):
    for axis, dim in sides:
        devices, length = (lax.axis_size(axis), array.shape[dim])
        up = [(i, (i + 1) % devices) for i in range(devices - 1)]
        down = [(j, i) for i, j in up]
        last = lax.slice_in_dim(array, length - width, length, axis=dim)
        first = lax.slice_in_dim(array, 0, width, axis=dim)
        before = lax.ppermute(last, axis, up)
        after = lax.ppermute(first, axis, down)
        array = jnp.concatenate([before, array, after], axis=dim)
    return array


def exact_dot(left_mat, right_mat):
    return jnp.dot(left_mat, right_mat, precision=HIGHEST, preferred_element_type=jnp.float32)


def time_embed(step_ids, model_width):
    half_width = model_width // 2
    frequency = jnp.exp(-math.log(10000.0) * jnp.arange(half_width, dtype=jnp.float32) / half_width)
    angles = step_ids.astype(jnp.float32)[:, None] * frequency[None, :]
    return jnp.concatenate([jnp.cos(angles), jnp.sin(angles)], axis=1)


def norm_rows(values):
    centered = values - jnp.mean(values, axis=1, keepdims=True)
    inverse = lax.rsqrt(jnp.mean(centered * centered, axis=1, keepdims=True) + NORM_EPS)
    return (centered * inverse, inverse)


def gelu_tanh(values):
    return jax.nn.gelu(values, approximate=True)


def local(
    tokens,
    out_grad,
    route_mask,
    kept_counts,
    labels,
    timesteps,
    class_table,
    ada_weight,
    ada_bias,
    qkv_weight,
    qv_bias,
    proj_weight,
    proj_bias,
    hidden_weight,
    hidden_bias,
    output_weight,
    output_bias,
):
    seq_index = lax.axis_index("seq")
    col_local = tokens.shape[1]
    model_width = class_table.shape[1]
    head_cols = qkv_weight.shape[2]
    heads_local = head_cols // HEAD_DIM
    window_imgs = 2 * IMG_DEV
    block_rows = min(512, K_ROWS)
    span_rows = block_rows + 2 * KEEP_MOST
    scale_factor = HEAD_DIM ** (-0.5)
    col_start = lax.axis_index("tp") * col_local
    image_ends = jnp.cumsum(kept_counts)
    first_image = seq_index * IMG_DEV
    before = jnp.where(seq_index > 0, image_ends[jnp.maximum(first_image - 1, 0)], 0)
    own_total = image_ends[first_image + IMG_DEV - 1] - before
    carry_in = before - seq_index * K_ROWS
    order_idx = jnp.argsort(1 - route_mask, stable=True)[: K_ROWS + SPILL]
    token_rank = jnp.clip(jnp.cumsum(route_mask) - 1, 0, K_ROWS + SPILL - 1)
    kept_flag = route_mask[:, None] > 0
    positions = seq_index * K_ROWS - KEEP_MOST + jnp.arange(K_ROWS + 2 * KEEP_MOST, dtype=jnp.int32)
    image_of = jnp.sum((image_ends[None, :] <= positions[:, None]).astype(jnp.int32), axis=1)
    key_image = jnp.where((positions >= 0) & (positions < image_ends[-1]), image_of, -1)
    row_image = key_image[KEEP_MOST : KEEP_MOST + K_ROWS]
    win_start = jnp.maximum(seq_index - 1, 0) * IMG_DEV
    row_onehot = (
        row_image[:, None] - win_start == jnp.arange(window_imgs, dtype=jnp.int32)[None, :]
    ).astype(jnp.float32)

    def regroup(compact):
        tail_rows = lax.dynamic_slice_in_dim(compact, own_total - SPILL, SPILL, 0)
        arrived = passed_along(tail_rows, "seq", 1)
        joined = jnp.concatenate([arrived, compact], axis=0)
        return lax.dynamic_slice_in_dim(joined, SPILL - carry_in, K_ROWS, 0)

    def reinsert(rows_new, initial):
        arrived = passed_along(rows_new[:SPILL], "seq", -1)
        joined = jnp.concatenate([rows_new, arrived, jnp.zeros_like(arrived)], axis=0)
        compact = lax.dynamic_slice_in_dim(joined, carry_in, K_ROWS + SPILL, 0)
        return jnp.where(kept_flag, compact[token_rank], initial)

    def whole_rows(part_rows):
        return lax.all_gather(part_rows, "tp", axis=1, tiled=True)

    def column_sum(part_rows):
        return lax.psum_scatter(
            part_rows.astype(jnp.bfloat16), "tp", scatter_dimension=1, tiled=True
        ).astype(jnp.float32)

    def own_cols(full_rows):
        return lax.dynamic_slice_in_dim(full_rows, col_start, col_local, 1)

    def input_grads(partial_rows, normed, inverse, scale):
        own_grad = lax.psum_scatter(
            partial_rows.astype(jnp.bfloat16), "tp", scatter_dimension=1, tiled=True
        ).astype(jnp.float32)
        normed_own = own_cols(normed)
        scaled_grad = own_grad * (1.0 + own_cols(scale))
        mean_grad, mean_cross = lax.psum(
            (
                jnp.sum(scaled_grad, axis=1, keepdims=True) / model_width,
                jnp.sum(scaled_grad * normed_own, axis=1, keepdims=True) / model_width,
            ),
            "tp",
        )
        return (
            own_grad,
            own_grad * normed_own,
            inverse * (scaled_grad - mean_grad - normed_own * mean_cross),
        )

    win_labels = lax.dynamic_slice_in_dim(labels, win_start, window_imgs)
    win_steps = lax.dynamic_slice_in_dim(timesteps, win_start, window_imgs)
    label_hot = (
        win_labels[:, None] == jnp.arange(class_table.shape[0], dtype=jnp.int32)[None, :]
    ).astype(jnp.bfloat16)
    condition = jnp.dot(label_hot, class_table, preferred_element_type=jnp.float32) + time_embed(
        win_steps, model_width
    )
    cond_low = jax.nn.silu(condition).astype(jnp.bfloat16)
    mod_own = (
        jnp.dot(
            cond_low,
            ada_weight.reshape(model_width, 6 * col_local),
            preferred_element_type=jnp.float32,
        ).reshape(window_imgs, 6, col_local)
        + ada_bias.astype(jnp.float32)[None]
    )
    mod_full = lax.all_gather(mod_own, "tp", axis=2, tiled=True)

    def row_full(stretch_id):
        return exact_dot(row_onehot, mod_full[:, stretch_id, :])

    def row_own(stretch_id):
        return exact_dot(row_onehot, mod_own[:, stretch_id, :])

    rows_in = regroup(tokens[order_idx])
    full_in = whole_rows(rows_in).astype(jnp.float32)
    normed_one, inverse_one = norm_rows(full_in)
    scale_one = row_full(1)
    branch_one = (normed_one * (1.0 + scale_one) + row_full(0)).astype(jnp.bfloat16)
    qkv_bias = jnp.stack([qv_bias[0], jnp.zeros_like(qv_bias[0]), qv_bias[1]]).astype(jnp.float32)
    qkv_rows = (
        jnp.einsum("rd,dcf->rcf", branch_one, qkv_weight, preferred_element_type=jnp.float32)
        + qkv_bias[None]
    ).astype(jnp.bfloat16)
    query_all = qkv_rows[:, 0].reshape(K_ROWS, heads_local, HEAD_DIM)
    window = padded(qkv_rows[:, 1:], (("seq", 0),), KEEP_MOST)
    window_keys = window[:, 0].reshape(-1, heads_local, HEAD_DIM)
    window_vals = window[:, 1].reshape(-1, heads_local, HEAD_DIM)

    def block_scores(block_index):
        start = block_index * block_rows
        raw = (
            jnp.einsum("qhe,khe->hqk", query_all, window_keys, preferred_element_type=jnp.float32)
            * scale_factor
        )
        same_image = (
            row_image[start : start + block_rows, None]
            == key_image[None, start : start + span_rows]
        )
        return jnp.where(same_image[None], raw, -1e30)

    block_index = 0
    start = block_index * block_rows
    masked = block_scores(block_index)
    top_score = jnp.max(masked, axis=2, keepdims=True)
    exp_scores = jnp.exp(masked - top_score)
    row_total = jnp.sum(exp_scores, axis=2, keepdims=True)
    attn_probs = (exp_scores / row_total).astype(jnp.bfloat16)
    lse_parts = [top_score + jnp.log(row_total)]
    attended_parts = jnp.einsum(
        "hqk,khe->qhe", attn_probs, window_vals, preferred_element_type=jnp.float32
    )
    attended = attended_parts.reshape(K_ROWS, head_cols).astype(jnp.bfloat16)
    attn_out = column_sum(
        jnp.dot(attended, proj_weight, preferred_element_type=jnp.float32)
    ) + proj_bias.astype(jnp.float32)
    gate_one = row_own(2)
    middle = rows_in.astype(jnp.float32) + gate_one * attn_out
    middle_full = whole_rows(middle.astype(jnp.bfloat16)).astype(jnp.float32)
    normed_two, inverse_two = norm_rows(middle_full)
    scale_two = row_full(4)
    branch_two = (normed_two * (1.0 + scale_two) + row_full(3)).astype(jnp.bfloat16)
    pre_act = jnp.dot(
        branch_two, hidden_weight, preferred_element_type=jnp.float32
    ) + hidden_bias.astype(jnp.float32)
    act_low = gelu_tanh(pre_act).astype(jnp.bfloat16)
    mlp_out = column_sum(
        jnp.dot(act_low, output_weight, preferred_element_type=jnp.float32)
    ) + output_bias.astype(jnp.float32)
    gate_two = row_own(5)
    final_rows = middle + gate_two * mlp_out
    output = reinsert(final_rows.astype(jnp.bfloat16), tokens)
    grad_rows = regroup(out_grad[order_idx]).astype(jnp.float32)
    gate_two_rows = grad_rows * mlp_out
    mlp_grad = (grad_rows * gate_two).astype(jnp.bfloat16)
    output_bias_term = jnp.sum(mlp_grad, axis=0, dtype=jnp.float32)
    mlp_grad_full = whole_rows(mlp_grad)
    output_weight_term = jnp.einsum(
        "rf,rd->fd", act_low, mlp_grad_full, preferred_element_type=jnp.float32
    )
    act_grad = jnp.einsum(
        "rd,fd->rf", mlp_grad_full, output_weight, preferred_element_type=jnp.float32
    )
    gelu_pull = jax.vjp(gelu_tanh, pre_act)[1]
    pre_grad = gelu_pull(act_grad)[0].astype(jnp.bfloat16)
    hidden_bias_term = jnp.sum(pre_grad, axis=0, dtype=jnp.float32)
    hidden_weight_term = jnp.einsum(
        "rd,rf->df", branch_two, pre_grad, preferred_element_type=jnp.float32
    )
    two_partial = jnp.einsum(
        "rf,df->rd", pre_grad, hidden_weight, preferred_element_type=jnp.float32
    )
    shift_two_grad, scale_two_grad, two_norm_grad = input_grads(
        two_partial, normed_two, inverse_two, scale_two
    )
    middle_grad = grad_rows + two_norm_grad
    gate_one_rows = middle_grad * attn_out
    attn_grad = (middle_grad * gate_one).astype(jnp.bfloat16)
    proj_bias_term = jnp.sum(attn_grad, axis=0, dtype=jnp.float32)
    attn_grad_full = whole_rows(attn_grad)
    proj_weight_term = jnp.einsum(
        "rf,rd->fd", attended, attn_grad_full, preferred_element_type=jnp.float32
    )
    attended_grad = (
        jnp.einsum("rd,fd->rf", attn_grad_full, proj_weight, preferred_element_type=jnp.float32)
        .astype(jnp.bfloat16)
        .reshape(K_ROWS, heads_local, HEAD_DIM)
    )
    window_grad = jnp.zeros((K_ROWS + 2 * KEEP_MOST, 2, heads_local, HEAD_DIM), jnp.float32)
    block_index = 0
    start = block_index * block_rows
    masked = block_scores(block_index)
    attn_probs = jnp.exp(masked - lse_parts[block_index])
    value_term = jnp.einsum(
        "hqk,qhe->khe",
        attn_probs.astype(jnp.bfloat16),
        attended_grad,
        preferred_element_type=jnp.float32,
    )
    prob_grad = jnp.einsum(
        "qhe,khe->hqk", attended_grad, window_vals, preferred_element_type=jnp.float32
    )
    row_dot = jnp.sum(attn_probs * prob_grad, axis=2, keepdims=True)
    score_grad = (attn_probs * (prob_grad - row_dot)).astype(jnp.bfloat16)
    query_parts = (
        jnp.einsum("hqk,khe->qhe", score_grad, window_keys, preferred_element_type=jnp.float32)
        * scale_factor
    )
    key_term = (
        jnp.einsum("hqk,qhe->khe", score_grad, query_all, preferred_element_type=jnp.float32)
        * scale_factor
    )
    window_grad = window_grad.at[start : start + span_rows].add(
        jnp.stack([key_term, value_term], axis=1)
    )
    from_right = passed_along(window_grad[:KEEP_MOST].astype(jnp.bfloat16), "seq", -1).astype(
        jnp.float32
    )
    from_left = passed_along(
        window_grad[K_ROWS + KEEP_MOST :].astype(jnp.bfloat16), "seq", 1
    ).astype(jnp.float32)
    own_kv = window_grad[KEEP_MOST : KEEP_MOST + K_ROWS]
    own_kv = own_kv.at[:KEEP_MOST].add(from_left).at[K_ROWS - KEEP_MOST :].add(from_right)
    qkv_grad = (
        jnp.concatenate([query_parts[:, None], own_kv], axis=1)
        .reshape(K_ROWS, 3, head_cols)
        .astype(jnp.bfloat16)
    )
    qkv_sums = jnp.sum(qkv_grad, axis=0, dtype=jnp.float32)
    qv_bias_term = jnp.stack([qkv_sums[0], qkv_sums[2]])
    qkv_weight_term = jnp.einsum(
        "rd,rcf->dcf", branch_one, qkv_grad, preferred_element_type=jnp.float32
    )
    one_partial = jnp.einsum(
        "rcf,dcf->rd", qkv_grad, qkv_weight, preferred_element_type=jnp.float32
    )
    shift_one_grad, scale_one_grad, one_norm_grad = input_grads(
        one_partial, normed_one, inverse_one, scale_one
    )
    in_grad = middle_grad + one_norm_grad
    tokens_grad = reinsert(in_grad.astype(jnp.bfloat16), out_grad)
    per_row = jnp.stack(
        [
            shift_one_grad,
            scale_one_grad,
            gate_one_rows,
            shift_two_grad,
            scale_two_grad,
            gate_two_rows,
        ],
        axis=1,
    )
    mod_grad = jnp.einsum(
        "rw,rcf->wcf", row_onehot, per_row, precision=HIGHEST, preferred_element_type=jnp.float32
    )
    ada_bias_term = jnp.sum(mod_grad, axis=0)
    ada_weight_term = jnp.einsum(
        "wd,wcf->dcf",
        cond_low.astype(jnp.float32),
        mod_grad,
        precision=HIGHEST,
        preferred_element_type=jnp.float32,
    )
    cond_grad = lax.psum(
        jnp.einsum(
            "wcf,dcf->wd",
            mod_grad,
            ada_weight.astype(jnp.float32),
            precision=HIGHEST,
            preferred_element_type=jnp.float32,
        ).astype(jnp.bfloat16),
        "tp",
    ).astype(jnp.float32)
    silu_pull = jax.vjp(jax.nn.silu, condition)[1]
    class_term = jnp.einsum(
        "wc,wd->cd",
        label_hot.astype(jnp.float32),
        silu_pull(cond_grad)[0],
        precision=HIGHEST,
        preferred_element_type=jnp.float32,
    )
    (
        ada_weight_grad,
        qkv_weight_grad,
        proj_weight_grad,
        hidden_weight_grad,
        output_weight_grad,
        class_grad,
    ) = (
        lax.psum_scatter(ada_weight_term, "seq", scatter_dimension=0, tiled=True),
        lax.psum_scatter(qkv_weight_term, "seq", scatter_dimension=0, tiled=True),
        lax.psum_scatter(proj_weight_term, "seq", scatter_dimension=1, tiled=True),
        lax.psum_scatter(hidden_weight_term, "seq", scatter_dimension=0, tiled=True),
        lax.psum_scatter(output_weight_term, "seq", scatter_dimension=1, tiled=True),
        lax.psum_scatter(class_term, "seq", scatter_dimension=1, tiled=True),
    )
    ada_bias_grad, qv_bias_grad, proj_bias_grad, hidden_bias_grad, output_bias_grad = lax.psum(
        (ada_bias_term, qv_bias_term, proj_bias_term, hidden_bias_term, output_bias_term), "seq"
    )
    return (
        output,
        tokens_grad,
        class_grad,
        ada_weight_grad,
        ada_bias_grad,
        qkv_weight_grad,
        qv_bias_grad,
        proj_weight_grad,
        proj_bias_grad,
        hidden_weight_grad,
        hidden_bias_grad,
        output_weight_grad,
        output_bias_grad,
    )


def solution(mesh):
    return jax.shard_map(
        local,
        mesh=mesh,
        in_specs=(
            P("seq", "tp"),
            P("seq", "tp"),
            P("seq"),
            P(),
            P(),
            P(),
            P(),
            P(None, None, "tp"),
            P(None, "tp"),
            P(None, None, "tp"),
            P(None, "tp"),
            P("tp", None),
            P("tp"),
            P(None, "tp"),
            P("tp"),
            P("tp", None),
            P("tp"),
        ),
        out_specs=(
            P("seq", "tp"),
            P("seq", "tp"),
            P(None, "seq"),
            P("seq", None, "tp"),
            P(None, "tp"),
            P("seq", None, "tp"),
            P(None, "tp"),
            P("tp", "seq"),
            P("tp"),
            P("seq", "tp"),
            P("tp"),
            P("tp", "seq"),
            P("tp"),
        ),
        check_vma=False,
    )
```

profile of v0, /device:TPU:0, one launch (start us, length us, event | category | flops | bytes accessed | tf_op | source)
XLA Modules:
  0.0 1055.8 jit_solution(1580755687282485058)
XLA Ops:
  9.4 4.4 sort.17
  25.2 5.5 collective-permute-start
  33.8 3.5 fusion.34
  38.7 39.6 %all_gather.16 = f32[8,6,1152]{1,0,2:T(8,128)} all-gather(f32[8,6,288]{1,0,2:T(8,128)} %copy.132), channel_id=1, replica_groups=mesh['seq'=8,'tp'=4] {'tp'}, dimensions={2}, use_global_device_ids=true | all-gather | bytes 276480 | tf_op jit(solution)/shard_map/all_gather | solution.py:161
  79.3 15.2 %fusion.94 = (f32[8,1,1152]{1,0,2:T(8,128)}, f32[8,1,1152]{1,0,2:T(8,128)}, f32[8,1,1152]{1,0,2:T(8,128)}, f32[8,1,1152]{1,0,2:T(8,128)}) fusion(f32[8,6,1152]{1,0,2:T(8,128)} %all_gather.16), kind=kLoop, calls=%fused_computation.195 | loop fusion | bytes 294912 | tf_op jit(solution)/shard_map/slice | solution.py:164
  95.8 3.9 copy.165
  99.7 3.9 copy.164
  107.0 3.3 fusion.67
  114.2 3.3 fusion.15
  119.0 3.9 collective-permute-start.1
  124.7 11.1 %collective-permute-done.1 = bf16[192,2,288]{0,2,1:T(8,128)(2,1)S(1)} collective-permute-done((bf16[192,2,288]{0,2,1:T(8,128)(2,1)S(1)}, bf16[192,2,288]{0,2,1:T(8,128)(2,1)S(1)}, u32[]{:S(2)}, u32[]{:S(2)}) %collective-permute-start.1) | collective-permute-done | bytes 221216 | tf_op jit(solution)/shard_map/ppermute | solution.py:29
  147.3 25.8 %reduce-scatter.11.cloned.1.call-done = bf16[512,288]{0,1:T(8,128)(2,1)} async-done(((bf16[512,1152]{0,1:T(8,128)(2,1)}), bf16[512,288]{0,1:T(8,128)(2,1)}) %reduce-scatter.11.cloned.1.call-update) | async-done | bytes 294928 | tf_op jit(solution)/shard_map/reduce_scatter | solution.py:118
  177.9 4.5 gather_fusion.2
  185.9 4.0 collective-permute-start.4
  191.2 3.9 copy.167
  195.1 3.9 copy.166
  202.5 3.3 fusion.64
  209.4 3.3 fusion.9
  218.2 5.9 convert_reduce_fusion.2
  227.9 4.6 convolution_convert_fusion.1
  232.6 3.3 fusion.13
  235.9 17.8 %reduce-scatter.15.cloned.1.call-done = bf16[512,288]{0,1:T(8,128)(2,1)} async-done(((bf16[512,1152]{0,1:T(8,128)(2,1)}), bf16[512,288]{0,1:T(8,128)(2,1)}) %reduce-scatter.15.cloned.1.call-update) | async-done | bytes 294928 | tf_op jit(solution)/shard_map/reduce_scatter | solution.py:126
  255.0 5.8 all-reduce.2
  260.8 21.1 %reduce-scatter.13.cloned.1.call-done = bf16[512,288]{0,1:T(8,128)(2,1)} async-done(((bf16[512,1152]{0,1:T(8,128)(2,1)}), bf16[512,288]{0,1:T(8,128)(2,1)}) %reduce-scatter.13.cloned.1.call-update) | async-done | bytes 294928 | tf_op jit(solution)/shard_map/reduce_scatter | solution.py:118
  285.4 17.4 %all-gather.11.cloned.1.call-done = bf16[512,1152]{0,1:T(8,128)(2,1)} async-done(((bf16[512,288]{0,1:T(8,128)(2,1)}), bf16[512,1152]{0,1:T(8,128)(2,1)}) %all-gather.11.cloned.1.call-update) | async-done | bytes 1179664 | tf_op jit(solution)/shard_map/all_gather | solution.py:115
  304.8 4.5 fusion.27
  309.4 4.6 multiply_reduce_fusion
  317.3 3.4 collective-permute-start.5
  327.6 3.5 scatter-add.6
  335.3 3.7 scatter-add.9
  340.3 4.2 fusion.10
  346.8 6.1 fusion.90
  354.2 5.3 fusion.104
  360.8 4.1 fusion.54
  368.0 3.4 reduce-scatter.17.cloned.1.call-done
  379.1 10.7 %psum.74 = bf16[8,1152]{1,0:T(8,128)(2,1)S(1)} all-reduce(bf16[8,1152]{1,0:T(8,128)(2,1)S(1)} %fusion.25), channel_id=1, replica_groups=mesh['seq'=8,'tp'=4] {'tp'}, use_global_device_ids=true, to_apply=%region_24.25 | all-reduce | flops 9216 | bytes 36864 | tf_op jit(solution)/shard_map/psum | solution.py:338
  389.8 4.4 fusion.59
  394.2 7.0 fusion.69
  407.9 6.3 all-reduce.1
  417.8 42.5 %all-reduce = (f32[6,288]{1,0:T(8,128)}, f32[2,288]{1,0:T(2,128)}, f32[288]{0:T(512)}, f32[1152]{0:T(1024)}, f32[288]{0:T(512)}) all-reduce(f32[6,288]{1,0:T(8,128)S(1)} %get-tuple-element.178, f32[2,288]{1,0:T(2,128)S(1)} %pad_maximum_fusion.5, f32[288]{0:T(512)S(1)} %get-tuple-element.142, ...), channel_id=1, replica_groups=mesh['seq'=8,'tp'=4] {'seq'}, use_global_device_ids=true, to_apply=%region_28.29 | all-reduce | flops 4032 | bytes 32256 | tf_op jit(solution)/shard_map/psum | solution.py:371
  462.6 5.0 gather_fusion.3
  467.5 5.0 gather_fusion.1
  472.6 3.3 broadcast_select_fusion
  480.3 69.1 %reduce-scatter.29.cloned.1.call-done = f32[1152,144]{0,1:T(8,128)} async-done(((f32[1152,1152]{0,1:T(8,128)}), f32[1152,144]{0,1:T(8,128)}) %reduce-scatter.29.cloned.1.call-update) | async-done | bytes 663568 | tf_op jit(solution)/shard_map/reduce_scatter | solution.py:368
  549.4 108.1 %reduce-scatter.27.cloned.1.call-done = f32[144,1152]{1,0:T(8,128)} async-done(((f32[1152,1152]{1,0:T(8,128)}), f32[144,1152]{1,0:T(8,128)}) %reduce-scatter.27.cloned.1.call-update) | async-done | bytes 663568 | tf_op jit(solution)/shard_map/reduce_scatter | solution.py:367
  657.5 108.3 %reduce-scatter.23.cloned.1.call-done = f32[144,3,288]{2,0,1:T(8,128)} async-done(((f32[1152,3,288]{2,0,1:T(8,128)}), f32[144,3,288]{2,0,1:T(8,128)}) %reduce-scatter.23.cloned.1.call-update) | async-done | bytes 497680 | tf_op jit(solution)/shard_map/reduce_scatter | solution.py:365
  765.8 99.3 %reduce-scatter.19.cloned.1.call-done = f32[1001,144]{0,1:T(8,128)} async-done(((f32[1001,1152]{0,1:T(8,128)}), f32[1001,144]{0,1:T(8,128)}) %reduce-scatter.19.cloned.1.call-update) | async-done | bytes 576592 | tf_op jit(solution)/shard_map/reduce_scatter | solution.py:369
  865.1 183.8 %reduce-scatter.21.cloned.1.call-done = f32[144,6,288]{2,0,1:T(8,128)} async-done(((f32[1152,6,288]{2,0,1:T(8,128)}), f32[144,6,288]{2,0,1:T(8,128)}) %reduce-scatter.21.cloned.1.call-update) | async-done | bytes 995344 | tf_op jit(solution)/shard_map/reduce_scatter | solution.py:364
  (292 shorter events, 121.7 us)
Async XLA Ops:
  7.2 211.0 %copy-start = (bf16[1152,1152]{1,0:T(8,128)(2,1)S(1)}, bf16[1152,1152]{1,0:T(8,128)(2,1)}, u32[]{:S(2)}) copy-start(bf16[1152,1152]{1,0:T(8,128)(2,1)} %param.40) | copy-start | bytes 7962628
  7.2 103.1 %all-gather.5.cloned.1.call-start = ((), (), s32[]{:S(2)}) async-start(), calls=%async_computation.10 | async-start | bytes 1474560 | tf_op jit(solution)/shard_map/all_gather | solution.py:115
  18.4 5.2 copy-start.40
  18.4 12.3 %copy-start.67 = (s32[32]{0:T(128)S(1)}, s32[32]{0:T(128)}, u32[]{:S(2)}) copy-start(s32[32]{0:T(128)} %param.29) | copy-start | bytes 388
  18.4 12.4 %copy-start.68 = (s32[32]{0:T(128)S(1)}, s32[32]{0:T(128)}, u32[]{:S(2)}) copy-start(s32[32]{0:T(128)} %param.30) | copy-start | bytes 388
  18.4 12.5 %copy-start.56 = (bf16[6,288]{1,0:T(8,128)(2,1)S(1)}, bf16[6,288]{1,0:T(8,128)(2,1)}, u32[]{:S(2)}) copy-start(bf16[6,288]{1,0:T(8,128)(2,1)} %param.33) | copy-start | bytes 10372
  25.2 53.1 %collective-permute-start = (bf16[128,288]{0,1:T(8,128)(2,1)}, bf16[128,288]{0,1:T(8,128)(2,1)}, u32[]{:S(2)}, u32[]{:S(2)}) collective-permute-start(bf16[128,288]{0,1:T(8,128)(2,1)} %constant_dynamic-slice_fusion.1), channel_id=1, source_target_pairs={{0,4},{4,8},{8,12},{12,16},{16,20},{20,24},{24,28},{1,5},{5,9},{9,... | collective-permute-start | bytes 221192 | tf_op jit(solution)/shard_map/ppermute | solution.py:19
  38.7 39.6 %copy-start.22 = (bf16[640,288]{0,1:T(8,128)(2,1)S(1)}, bf16[640,288]{0,1:T(8,128)(2,1)}, u32[]{:S(2)}) copy-start(bf16[640,288]{0,1:T(8,128)(2,1)} %copy.130) | copy-start | bytes 1105924
  79.2 93.8 %reduce-scatter.11.cloned.1.call-start = ((), (), s32[]{:S(2)}) async-start(), calls=%async_computation.11 | async-start | bytes 1474560 | tf_op jit(solution)/shard_map/reduce_scatter | solution.py:118
  117.5 6.8 copy-start.50
  117.5 6.8 copy-start.52
  119.0 16.8 %collective-permute-start.1 = (bf16[192,2,288]{0,2,1:T(8,128)(2,1)S(1)}, bf16[192,2,288]{0,2,1:T(8,128)(2,1)S(1)}, u32[]{:S(2)}, u32[]{:S(2)}) collective-permute-start(bf16[192,2,288]{0,2,1:T(8,128)(2,1)S(1)} %get-tuple-element.153), channel_id=1, source_target_pairs={{0,4},{4,8},{8,12},{12,16},{16,20},{20,24},{24,28},{1,5},{5,9},{9,... | collective-permute-start | bytes 663560 | tf_op jit(solution)/shard_map/ppermute | solution.py:29
  123.0 12.9 %collective-permute-start.2 = (bf16[192,2,288]{0,2,1:T(8,128)(2,1)S(1)}, bf16[192,2,288]{0,2,1:T(8,128)(2,1)S(1)}, u32[]{:S(2)}, u32[]{:S(2)}) collective-permute-start(bf16[192,2,288]{0,2,1:T(8,128)(2,1)S(1)} %get-tuple-element.154), channel_id=1, source_target_pairs={{4,0},{8,4},{12,8},{16,12},{20,16},{24,20},{28,24},{5,1},{9,5},{13... | collective-permute-start | bytes 663560 | tf_op jit(solution)/shard_map/ppermute | solution.py:30
  124.7 11.8 %copy-start.15 = (bf16[512,1,288]{0,2,1:T(8,128)(2,1)}, bf16[512,1,288]{0,2,1:T(8,128)(2,1)S(1)}, u32[]{:S(2)}) copy-start(bf16[512,1,288]{0,2,1:T(8,128)(2,1)S(1)} %slice.212) | copy-start | bytes 884740
  146.0 59.9 %all-gather.7.cloned.1.call-start = ((), (), s32[]{:S(2)}) async-start(), calls=%async_computation.12 | async-start | bytes 1474560 | tf_op jit(solution)/shard_map/all_gather | solution.py:115
  175.6 42.6 %all-gather.9.cloned.1.call-start = ((), (), s32[]{:S(2)}) async-start(), calls=%async_computation.14 | async-start | bytes 1474560 | tf_op jit(solution)/shard_map/all_gather | solution.py:115
  185.9 13.1 %collective-permute-start.4 = (bf16[128,288]{0,1:T(8,128)(2,1)}, bf16[128,288]{0,1:T(8,128)(2,1)}, u32[]{:S(2)}, u32[]{:S(2)}) collective-permute-start(bf16[128,288]{0,1:T(8,128)(2,1)} %constant_dynamic-slice_fusion), channel_id=1, source_target_pairs={{0,4},{4,8},{8,12},{12,16},{16,20},{20,24},{24,28},{1,5},{5,9},{9,... | collective-permute-start | bytes 221192 | tf_op jit(solution)/shard_map/ppermute | solution.py:19
  202.1 7.2 copy-start.33
  202.1 51.6 %reduce-scatter.15.cloned.1.call-start = ((), (), s32[]{:S(2)}) async-start(), calls=%async_computation.15 | async-start | bytes 1474560 | tf_op jit(solution)/shard_map/reduce_scatter | solution.py:126
  218.2 6.9 copy-start.64
  227.9 54.0 %reduce-scatter.13.cloned.1.call-start = ((), (), s32[]{:S(2)}) async-start(), calls=%async_computation.13 | async-start | bytes 1474560 | tf_op jit(solution)/shard_map/reduce_scatter | solution.py:118
  232.5 21.2 %copy-start.7 = (f32[512,1152]{0,1:T(8,128)S(1)}, f32[512,1152]{0,1:T(8,128)}, u32[]{:S(2)}) copy-start(f32[512,1152]{0,1:T(8,128)} %fusion.64) | copy-start | bytes 7077892
  232.5 70.2 %all-gather.11.cloned.1.call-start = ((), (), s32[]{:S(2)}) async-start(), calls=%async_computation.16 | async-start | bytes 1474560 | tf_op jit(solution)/shard_map/all_gather | solution.py:115
  232.6 49.3 %copy-start.10 = (bf16[512,288]{0,1:T(8,128)(2,1)S(1)}, bf16[512,288]{0,1:T(8,128)(2,1)}, u32[]{:S(2)}) copy-start(bf16[512,288]{0,1:T(8,128)(2,1)} %fusion.53) | copy-start | bytes 884740
  232.6 49.3 %copy-start.46 = (f32[288]{0:T(512)S(1)}, f32[288]{0:T(512)}, u32[]{:S(2)}) copy-start(f32[288]{0:T(512)} %convert_element_type.162) | copy-start | bytes 3460
  285.1 86.2 %reduce-scatter.17.cloned.1.call-start = ((), (), s32[]{:S(2)}) async-start(), calls=%async_computation.17 | async-start | bytes 1474560 | tf_op jit(solution)/shard_map/reduce_scatter | solution.py:126
  304.8 9.2 slice-start
  317.3 10.0 collective-permute-start.5
  322.8 11.1 %collective-permute-start.6 = (bf16[192,2,4,72]{0,3,2,1:T(8,128)(2,1)}, bf16[192,2,4,72]{0,3,2,1:T(8,128)(2,1)}, u32[]{:S(2)}, u32[]{:S(2)}) collective-permute-start(bf16[192,2,4,72]{0,3,2,1:T(8,128)(2,1)} %get-tuple-element.149), channel_id=1, source_target_pairs={{4,0},{8,4},{12,8},{16,12},{20,16},{24,20},{28,24},{5,1},{9,5},{13... | collective-permute-start | bytes 663560 | tf_op jit(solution)/shard_map/ppermute | solution.py:19
  331.1 9.2 copy-start.24
  340.3 19.6 %copy-start.19 = (bf16[512,2,4,72]{0,3,2,1:T(8,128)(2,1)}, bf16[512,2,4,72]{0,3,2,1:T(8,128)(2,1)S(1)}, u32[]{:S(2)}) copy-start(bf16[512,2,4,72]{0,3,2,1:T(8,128)(2,1)S(1)} %convert.15) | copy-start | bytes 1769476
  344.6 135.7 %reduce-scatter.25.cloned.1.call-start = ((), (), s32[]{:S(2)}) async-start(), calls=%async_computation.21 | async-start | bytes 1990656 | tf_op jit(solution)/shard_map/reduce_scatter | solution.py:366
  346.7 202.6 %reduce-scatter.29.cloned.1.call-start = ((), (), s32[]{:S(2)}) async-start(), calls=%async_computation.23 | async-start | bytes 5971968 | tf_op jit(solution)/shard_map/reduce_scatter | solution.py:368
  352.9 304.5 %reduce-scatter.27.cloned.1.call-start = ((), (), s32[]{:S(2)}) async-start(), calls=%async_computation.22 | async-start | bytes 5971968 | tf_op jit(solution)/shard_map/reduce_scatter | solution.py:367
  359.6 406.2 %reduce-scatter.23.cloned.1.call-start = ((), (), s32[]{:S(2)}) async-start(), calls=%async_computation.20 | async-start | bytes 5971968 | tf_op jit(solution)/shard_map/reduce_scatter | solution.py:365
  365.0 8.7 copy-start.9
  365.0 8.7 copy-start.17
  365.0 500.1 %reduce-scatter.19.cloned.1.call-start = ((), (), s32[]{:S(2)}) async-start(), calls=%async_computation.18 | async-start | bytes 5308416 | tf_op jit(solution)/shard_map/reduce_scatter | solution.py:369
  368.0 5.9 copy-start.11
  377.1 12.6 %copy-start.61 = (s32[8]{0:T(128)S(1)}, s32[8]{0:T(128)}, u32[]{:S(2)}) copy-start(s32[8]{0:T(128)} %copy-done.60) | copy-start | bytes 100
  394.1 654.7 %reduce-scatter.21.cloned.1.call-start = ((), (), s32[]{:S(2)}) async-start(), calls=%async_computation.19 | async-start | bytes 11943936 | tf_op jit(solution)/shard_map/reduce_scatter | solution.py:364
  401.2 5.5 copy-start.8
  401.2 5.5 copy-start.12
  403.3 14.5 %copy-start.51 = (f32[288]{0:T(512)S(1)}, f32[288]{0:T(512)}, u32[]{:S(2)}) copy-start(f32[288]{0:T(512)} %get-tuple-element.137) | copy-start | bytes 3460
  403.3 57.0 %collective-permute-start.3 = (bf16[128,288]{0,1:T(8,128)(2,1)S(1)}, bf16[128,288]{0,1:T(8,128)(2,1)}, u32[]{:S(2)}, u32[]{:S(2)}) collective-permute-start(bf16[128,288]{0,1:T(8,128)(2,1)S(1)} %slice.217), channel_id=1, source_target_pairs={{4,0},{8,4},{12,8},{16,12},{20,16},{24,20},{28,24},{5,1},{9,5},{13... | collective-permute-start | bytes 221192 | tf_op jit(solution)/shard_map/ppermute | solution.py:19
  414.2 48.3 %copy-start.39 = (s32[1024]{0:T(1024)S(1)}, s32[1024]{0:T(1024)}, u32[]{:S(2)}) copy-start(s32[1024]{0:T(1024)} %get-tuple-element.181) | copy-start | bytes 12292
  416.5 43.9 %collective-permute-start.7 = (bf16[128,288]{0,1:T(8,128)(2,1)S(1)}, bf16[128,288]{0,1:T(8,128)(2,1)S(1)}, u32[]{:S(2)}, u32[]{:S(2)}) collective-permute-start(bf16[128,288]{0,1:T(8,128)(2,1)S(1)} %slice.226), channel_id=1, source_target_pairs={{4,0},{8,4},{12,8},{16,12},{20,16},{24,20},{28,24},{5,1},{9,5},{13... | collective-permute-start | bytes 221192 | tf_op jit(solution)/shard_map/ppermute | solution.py:19
  472.6 576.3 %copy-start.1 = (bf16[1152,1152]{1,0:T(8,128)(2,1)S(1)}, bf16[1152,1152]{1,0:T(8,128)(2,1)}, u32[]{:S(2)}) copy-start(bf16[1152,1152]{1,0:T(8,128)(2,1)} %param.40) | copy-start | bytes 7962628
  (46 other events, 123.8 us)
Sparse Core Ops, SparseCore 0:
  79.3 17.1 all-gather.4
  146.1 26.9 reduce-scatter.10
  175.7 17.4 all-gather.6
  202.2 15.9 all-gather.8
  228.0 25.7 reduce-scatter.14
  256.1 25.7 reduce-scatter.12
  285.3 17.4 all-gather.10
  344.7 26.5 reduce-scatter.16
  375.4 66.5 reduce-scatter.24
  446.5 102.8 reduce-scatter.28
  553.5 103.9 reduce-scatter.26
  661.9 103.8 reduce-scatter.22
  770.0 95.0 reduce-scatter.18
  869.1 179.6 reduce-scatter.20
where the time goes:
time: 1070 us; the launch traced here: 1060 us
  waiting for transfers between devices  671 us (63%)
  blocking collectives  105 us (10%)
  matrix products  98.7 us (9%)
  local copies, waits for them, and re-layouts  87.5 us (8%)
  other arithmetic  53.5 us (5%)
  starting transfers between devices  23.5 us (2%)
  between operations  16.7 us (2%)
    reduce_scatter x1, waiting for transfers between devices, local(): lax.psum_scatter(ada_weight_term, 'seq', scatter_dimension=0, tiled=True)  184 us
    reduce_scatter x1, waiting for transfers between devices, local(): lax.psum_scatter(qkv_weight_term, 'seq', scatter_dimension=0, tiled=True)  108 us
    reduce_scatter x1, waiting for transfers between devices, local(): lax.psum_scatter(hidden_weight_term, 'seq', scatter_dimension=0, tiled=True)  108 us
    reduce_scatter x1, waiting for transfers between devices, local(): lax.psum_scatter(class_term, 'seq', scatter_dimension=1, tiled=True)  99.3 us
    reduce_scatter x1, waiting for transfers between devices, local(): lax.psum_scatter(output_weight_term, 'seq', scatter_dimension=1, tiled=True)  69.1 us
    reduce_scatter x2, waiting for transfers between devices, column_sum(): lax.psum_scatter(part_rows.astype(jnp.bfloat16), 'tp', scatter_dimension=...  46.9 us
    psum x1, blocking collectives, local(): lax.psum((ada_bias_term, qv_bias_term, proj_bias_term, hidden_bias_term,...  42.5 us
    all_gather x1, blocking collectives, local(): mod_full = lax.all_gather(mod_own, 'tp', axis=2, tiled=True)  39.6 us
  transfers between devices with their start and end apart: 22, of which 14 were waited for; matrix products, arithmetic and copies ran while one was open for 15% of the time, Pallas kernels for 0%

commit v1 on v0

--- a/solution.py
+++ b/solution.py
@@ -158,7 +158,12 @@
         ).reshape(window_imgs, 6, col_local)
         + ada_bias.astype(jnp.float32)[None]
     )
-    mod_full = lax.all_gather(mod_own, "tp", axis=2, tiled=True)
+    ring = [mod_own]
+    for hop in range(3):
+        ring.append(lax.ppermute(ring[-1], "tp", [(dev, (dev + 1) % 4) for dev in range(4)]))
+    mod_full = jnp.roll(
+        jnp.concatenate(ring[::-1], axis=2), (lax.axis_index("tp") + 1) * ring[0].shape[2], axis=2
+    )
 
     def row_full(stretch_id):
         return exact_dot(row_onehot, mod_full[:, stretch_id, :])

time: 1070 us -> 1010 us (0.944)
  blocking collectives: 105 us -> 64.9 us
  local copies, waits for them, and re-layouts: 87.5 us -> 58.5 us
  waiting for transfers between devices: 671 us -> 682 us
    all_gather x1 -> x0, blocking collectives: 39.6 us -> none  [local(): mod_full = lax.all_gather(mod_own, 'tp', axis=2, tiled=True)]
    unnamed x152 -> x142, local copies, waits for them, and re-layouts: 34.1 us -> 17.8 us
    slice x1 -> x0, local copies, waits for them, and re-layouts: 15.2 us -> none  [row_full(): return exact_dot(row_onehot, mod_full[:, stretch_id, :])]
  transfers between devices with their start and end apart: 22 -> 25, of which waited for: 14 -> 18; matrix products, arithmetic and copies ran while one was open for 15% -> 13% of each run, Pallas kernels for 0% -> 0%
where the time goes in v1:
time: 1010 us; the launch traced here: 1000 us
  waiting for transfers between devices  682 us (68%)
  matrix products  101 us (10%)
  blocking collectives  64.9 us (6%)
  local copies, waits for them, and re-layouts  58.5 us (6%)
  other arithmetic  55.5 us (5%)
  starting transfers between devices  22.7 us (2%)
  between operations  16.5 us (2%)
    reduce_scatter x1, waiting for transfers between devices, local(): lax.psum_scatter(ada_weight_term, 'seq', scatter_dimension=0, tiled=True)  184 us
    reduce_scatter x1, waiting for transfers between devices, local(): lax.psum_scatter(qkv_weight_term, 'seq', scatter_dimension=0, tiled=True)  108 us
    reduce_scatter x1, waiting for transfers between devices, local(): lax.psum_scatter(hidden_weight_term, 'seq', scatter_dimension=0, tiled=True)  108 us
    reduce_scatter x1, waiting for transfers between devices, local(): lax.psum_scatter(class_term, 'seq', scatter_dimension=1, tiled=True)  99.3 us
    reduce_scatter x1, waiting for transfers between devices, local(): lax.psum_scatter(output_weight_term, 'seq', scatter_dimension=1, tiled=True)  67.6 us
    reduce_scatter x2, waiting for transfers between devices, column_sum(): lax.psum_scatter(part_rows.astype(jnp.bfloat16), 'tp', scatter_dimension=...  48.6 us
    psum x1, blocking collectives, local(): lax.psum((ada_bias_term, qv_bias_term, proj_bias_term, hidden_bias_term,...  42.1 us
    reduce_scatter x2, waiting for transfers between devices, input_grads(): lax.psum_scatter(partial_rows.astype(jnp.bfloat16), 'tp', scatter_dimensi...  21.2 us
  transfers between devices with their start and end apart: 25, of which 18 were waited for; matrix products, arithmetic and copies ran while one was open for 13% of the time, Pallas kernels for 0%

profile of v1, /device:TPU:0, one launch (start us, length us, event | category | flops | bytes accessed | tf_op | source)
XLA Modules:
  0.0 1001.4 jit_solution(13797660277068683009)
XLA Ops:
  9.4 4.4 sort.17
  18.4 3.2 gather_fusion
  25.2 4.9 collective-permute-start
  37.0 3.5 fusion.34
  45.2 4.6 collective-permute-done.2
  50.5 3.6 collective-permute-done.3
  56.1 3.6 fusion.64
  63.6 3.7 fusion.15
  68.8 3.6 collective-permute-start.4
  74.3 10.2 %collective-permute-done.4 = bf16[192,2,288]{0,2,1:T(8,128)(2,1)S(1)} collective-permute-done((bf16[192,2,288]{0,2,1:T(8,128)(2,1)S(1)}, bf16[192,2,288]{0,2,1:T(8,128)(2,1)S(1)}, u32[]{:S(2)}, u32[]{:S(2)}) %collective-permute-start.4) | collective-permute-done | bytes 221216 | tf_op jit(solution)/shard_map/ppermute | solution.py:29
  95.9 27.6 %reduce-scatter.11.cloned.1.call-done = bf16[512,288]{0,1:T(8,128)(2,1)} async-done(((bf16[512,1152]{0,1:T(8,128)(2,1)}), bf16[512,288]{0,1:T(8,128)(2,1)}) %reduce-scatter.11.cloned.1.call-update) | async-done | bytes 294928 | tf_op jit(solution)/shard_map/reduce_scatter | solution.py:118
  128.3 4.5 gather_fusion.2
  136.3 4.0 collective-permute-start.7
  145.3 3.6 fusion.63
  152.2 3.9 fusion.9
  157.2 3.2 convolution_add_fusion.2
  160.3 3.2 all-gather.9.cloned.1.call-done
  163.6 5.9 convert_reduce_fusion.2
  173.3 4.5 convolution_convert_fusion.1
  177.9 3.3 fusion.13
  181.2 17.8 %reduce-scatter.15.cloned.1.call-done = bf16[512,288]{0,1:T(8,128)(2,1)} async-done(((bf16[512,1152]{0,1:T(8,128)(2,1)}), bf16[512,288]{0,1:T(8,128)(2,1)}) %reduce-scatter.15.cloned.1.call-update) | async-done | bytes 294928 | tf_op jit(solution)/shard_map/reduce_scatter | solution.py:126
  200.4 5.8 all-reduce.2
  206.2 21.1 %reduce-scatter.13.cloned.1.call-done = bf16[512,288]{0,1:T(8,128)(2,1)} async-done(((bf16[512,1152]{0,1:T(8,128)(2,1)}), bf16[512,288]{0,1:T(8,128)(2,1)}) %reduce-scatter.13.cloned.1.call-update) | async-done | bytes 294928 | tf_op jit(solution)/shard_map/reduce_scatter | solution.py:118
  227.3 3.8 convert_reduce_fusion.5
  231.5 17.1 %all-gather.11.cloned.1.call-done = bf16[512,1152]{0,1:T(8,128)(2,1)} async-done(((bf16[512,288]{0,1:T(8,128)(2,1)}), bf16[512,1152]{0,1:T(8,128)(2,1)}) %all-gather.11.cloned.1.call-update) | async-done | bytes 1179664 | tf_op jit(solution)/shard_map/all_gather | solution.py:115
  250.7 4.5 fusion.27
  255.3 4.6 multiply_reduce_fusion
  263.3 3.4 collective-permute-start.8
  273.5 3.5 scatter-add.6
  281.2 3.7 scatter-add.9
  286.3 4.2 fusion.10
  292.7 6.1 fusion.90
  300.2 5.3 fusion.103
  306.8 4.1 fusion.54
  313.9 3.4 reduce-scatter.17.cloned.1.call-done
  325.5 10.3 %psum.74 = bf16[8,1152]{1,0:T(8,128)(2,1)S(1)} all-reduce(bf16[8,1152]{1,0:T(8,128)(2,1)S(1)} %fusion.25), channel_id=1, replica_groups=mesh['seq'=8,'tp'=4] {'tp'}, use_global_device_ids=true, to_apply=%region_24.25 | all-reduce | flops 9216 | bytes 36864 | tf_op jit(solution)/shard_map/psum | solution.py:343
  335.8 4.3 fusion.59
  340.2 7.0 fusion.65
  355.2 6.8 all-reduce.1
  365.6 42.1 %all-reduce = (f32[6,288]{1,0:T(8,128)}, f32[2,288]{1,0:T(2,128)}, f32[288]{0:T(512)}, f32[1152]{0:T(1024)}, f32[288]{0:T(512)}) all-reduce(f32[6,288]{1,0:T(8,128)S(1)} %copy-done.35, f32[2,288]{1,0:T(2,128)S(1)} %pad_maximum_fusion.5, f32[288]{0:T(512)S(1)} %copy-done.50, ...), channel_id=1, replica_groups=mesh['seq'=8,'tp'=4] {'seq'}, use_global_device_ids=true, to_apply=%region_28.29 | all-reduce | flops 4032 | bytes 32256 | tf_op jit(solution)/shard_map/psum | solution.py:376
  409.9 5.0 gather_fusion.3
  414.9 5.0 gather_fusion.1
  419.9 3.3 broadcast_select_fusion
  427.6 67.6 %reduce-scatter.29.cloned.1.call-done = f32[1152,144]{0,1:T(8,128)} async-done(((f32[1152,1152]{0,1:T(8,128)}), f32[1152,144]{0,1:T(8,128)}) %reduce-scatter.29.cloned.1.call-update) | async-done | bytes 663568 | tf_op jit(solution)/shard_map/reduce_scatter | solution.py:373
  495.2 108.1 %reduce-scatter.27.cloned.1.call-done = f32[144,1152]{1,0:T(8,128)} async-done(((f32[1152,1152]{1,0:T(8,128)}), f32[144,1152]{1,0:T(8,128)}) %reduce-scatter.27.cloned.1.call-update) | async-done | bytes 663568 | tf_op jit(solution)/shard_map/reduce_scatter | solution.py:372
  603.3 108.3 %reduce-scatter.23.cloned.1.call-done = f32[144,3,288]{2,0,1:T(8,128)} async-done(((f32[1152,3,288]{2,0,1:T(8,128)}), f32[144,3,288]{2,0,1:T(8,128)}) %reduce-scatter.23.cloned.1.call-update) | async-done | bytes 497680 | tf_op jit(solution)/shard_map/reduce_scatter | solution.py:370
  711.6 99.3 %reduce-scatter.19.cloned.1.call-done = f32[1001,144]{0,1:T(8,128)} async-done(((f32[1001,1152]{0,1:T(8,128)}), f32[1001,144]{0,1:T(8,128)}) %reduce-scatter.19.cloned.1.call-update) | async-done | bytes 576592 | tf_op jit(solution)/shard_map/reduce_scatter | solution.py:374
  810.9 183.8 %reduce-scatter.21.cloned.1.call-done = f32[144,6,288]{2,0,1:T(8,128)} async-done(((f32[1152,6,288]{2,0,1:T(8,128)}), f32[144,6,288]{2,0,1:T(8,128)}) %reduce-scatter.21.cloned.1.call-update) | async-done | bytes 995344 | tf_op jit(solution)/shard_map/reduce_scatter | solution.py:369
  (286 shorter events, 116.9 us)
Async XLA Ops:
  7.2 156.4 %copy-start = (bf16[1152,1152]{1,0:T(8,128)(2,1)S(1)}, bf16[1152,1152]{1,0:T(8,128)(2,1)}, u32[]{:S(2)}) copy-start(bf16[1152,1152]{1,0:T(8,128)(2,1)} %param.40) | copy-start | bytes 7962628
  7.2 52.5 %all-gather.5.cloned.1.call-start = ((), (), s32[]{:S(2)}) async-start(), calls=%async_computation.10 | async-start | bytes 1474560 | tf_op jit(solution)/shard_map/all_gather | solution.py:115
  18.4 12.3 %copy-start.65 = (s32[32]{0:T(128)S(1)}, s32[32]{0:T(128)}, u32[]{:S(2)}) copy-start(s32[32]{0:T(128)} %param.30) | copy-start | bytes 388
  25.2 7.7 collective-permute-start
  34.8 88.7 %reduce-scatter.11.cloned.1.call-start = ((), (), s32[]{:S(2)}) async-start(), calls=%async_computation.11 | async-start | bytes 1474560 | tf_op jit(solution)/shard_map/reduce_scatter | solution.py:118
  40.4 3.9 collective-permute-start.1
  44.3 5.5 collective-permute-start.2
  49.8 4.2 collective-permute-start.3
  67.3 6.6 copy-start.48
  67.3 6.6 copy-start.51
  68.8 15.6 %collective-permute-start.4 = (bf16[192,2,288]{0,2,1:T(8,128)(2,1)S(1)}, bf16[192,2,288]{0,2,1:T(8,128)(2,1)S(1)}, u32[]{:S(2)}, u32[]{:S(2)}) collective-permute-start(bf16[192,2,288]{0,2,1:T(8,128)(2,1)S(1)} %get-tuple-element.123), channel_id=1, source_target_pairs={{0,4},{4,8},{8,12},{12,16},{16,20},{20,24},{24,28},{1,5},{5,9},{9,... | collective-permute-start | bytes 663560 | tf_op jit(solution)/shard_map/ppermute | solution.py:29
  72.4 12.1 %collective-permute-start.5 = (bf16[192,2,288]{0,2,1:T(8,128)(2,1)S(1)}, bf16[192,2,288]{0,2,1:T(8,128)(2,1)S(1)}, u32[]{:S(2)}, u32[]{:S(2)}) collective-permute-start(bf16[192,2,288]{0,2,1:T(8,128)(2,1)S(1)} %get-tuple-element.124), channel_id=1, source_target_pairs={{4,0},{8,4},{12,8},{16,12},{20,16},{24,20},{28,24},{5,1},{9,5},{13... | collective-permute-start | bytes 663560 | tf_op jit(solution)/shard_map/ppermute | solution.py:30
  74.2 10.8 %copy-start.15 = (bf16[512,1,288]{0,2,1:T(8,128)(2,1)}, bf16[512,1,288]{0,2,1:T(8,128)(2,1)S(1)}, u32[]{:S(2)}) copy-start(bf16[512,1,288]{0,2,1:T(8,128)(2,1)S(1)} %slice.210) | copy-start | bytes 884740
  94.6 54.4 %all-gather.7.cloned.1.call-start = ((), (), s32[]{:S(2)}) async-start(), calls=%async_computation.12 | async-start | bytes 1474560 | tf_op jit(solution)/shard_map/all_gather | solution.py:115
  125.9 37.6 %all-gather.9.cloned.1.call-start = ((), (), s32[]{:S(2)}) async-start(), calls=%async_computation.14 | async-start | bytes 1474560 | tf_op jit(solution)/shard_map/all_gather | solution.py:115
  136.3 5.7 collective-permute-start.7
  145.0 54.0 %reduce-scatter.15.cloned.1.call-start = ((), (), s32[]{:S(2)}) async-start(), calls=%async_computation.15 | async-start | bytes 1474560 | tf_op jit(solution)/shard_map/reduce_scatter | solution.py:126
  163.5 6.9 copy-start.62
  173.2 54.0 %reduce-scatter.13.cloned.1.call-start = ((), (), s32[]{:S(2)}) async-start(), calls=%async_computation.13 | async-start | bytes 1474560 | tf_op jit(solution)/shard_map/reduce_scatter | solution.py:118
  177.8 21.3 %copy-start.7 = (f32[512,1152]{0,1:T(8,128)S(1)}, f32[512,1152]{0,1:T(8,128)}, u32[]{:S(2)}) copy-start(f32[512,1152]{0,1:T(8,128)} %fusion.63) | copy-start | bytes 7077892
  177.8 70.8 %all-gather.11.cloned.1.call-start = ((), (), s32[]{:S(2)}) async-start(), calls=%async_computation.16 | async-start | bytes 1474560 | tf_op jit(solution)/shard_map/all_gather | solution.py:115
  177.9 49.4 %copy-start.10 = (bf16[512,288]{0,1:T(8,128)(2,1)S(1)}, bf16[512,288]{0,1:T(8,128)(2,1)}, u32[]{:S(2)}) copy-start(bf16[512,288]{0,1:T(8,128)(2,1)} %fusion.53) | copy-start | bytes 884740
  177.9 49.4 %copy-start.44 = (f32[288]{0:T(512)S(1)}, f32[288]{0:T(512)}, u32[]{:S(2)}) copy-start(f32[288]{0:T(512)} %convert_element_type.162) | copy-start | bytes 3460
  231.1 86.2 %reduce-scatter.17.cloned.1.call-start = ((), (), s32[]{:S(2)}) async-start(), calls=%async_computation.17 | async-start | bytes 1474560 | tf_op jit(solution)/shard_map/reduce_scatter | solution.py:126
  250.7 9.2 slice-start
  263.3 10.0 %collective-permute-start.8 = (bf16[192,2,4,72]{0,3,2,1:T(8,128)(2,1)S(1)}, bf16[192,2,4,72]{0,3,2,1:T(8,128)(2,1)S(1)}, u32[]{:S(2)}, u32[]{:S(2)}) collective-permute-start(bf16[192,2,4,72]{0,3,2,1:T(8,128)(2,1)S(1)} %get-tuple-element.120), channel_id=1, source_target_pairs={{0,4},{4,8},{8,12},{12,16},{16,20},{20,24},{24,28},{1,5},{5,9},{9,... | collective-permute-start | bytes 663560 | tf_op jit(solution)/shard_map/ppermute | solution.py:19
  268.8 11.1 %collective-permute-start.9 = (bf16[192,2,4,72]{0,3,2,1:T(8,128)(2,1)}, bf16[192,2,4,72]{0,3,2,1:T(8,128)(2,1)}, u32[]{:S(2)}, u32[]{:S(2)}) collective-permute-start(bf16[192,2,4,72]{0,3,2,1:T(8,128)(2,1)} %get-tuple-element.119), channel_id=1, source_target_pairs={{4,0},{8,4},{12,8},{16,12},{20,16},{24,20},{28,24},{5,1},{9,5},{13... | collective-permute-start | bytes 663560 | tf_op jit(solution)/shard_map/ppermute | solution.py:19
  277.0 9.2 copy-start.23
  286.2 19.5 %copy-start.19 = (bf16[512,2,4,72]{0,3,2,1:T(8,128)(2,1)}, bf16[512,2,4,72]{0,3,2,1:T(8,128)(2,1)S(1)}, u32[]{:S(2)}) copy-start(bf16[512,2,4,72]{0,3,2,1:T(8,128)(2,1)S(1)} %convert.15) | copy-start | bytes 1769476
  290.5 137.1 %reduce-scatter.25.cloned.1.call-start = ((), (), s32[]{:S(2)}) async-start(), calls=%async_computation.21 | async-start | bytes 1990656 | tf_op jit(solution)/shard_map/reduce_scatter | solution.py:371
  292.7 202.5 %reduce-scatter.29.cloned.1.call-start = ((), (), s32[]{:S(2)}) async-start(), calls=%async_computation.23 | async-start | bytes 5971968 | tf_op jit(solution)/shard_map/reduce_scatter | solution.py:373
  298.9 304.5 %reduce-scatter.27.cloned.1.call-start = ((), (), s32[]{:S(2)}) async-start(), calls=%async_computation.22 | async-start | bytes 5971968 | tf_op jit(solution)/shard_map/reduce_scatter | solution.py:372
  305.5 406.1 %reduce-scatter.23.cloned.1.call-start = ((), (), s32[]{:S(2)}) async-start(), calls=%async_computation.20 | async-start | bytes 5971968 | tf_op jit(solution)/shard_map/reduce_scatter | solution.py:370
  310.9 8.7 copy-start.9
  310.9 8.7 copy-start.17
  310.9 500.0 %reduce-scatter.19.cloned.1.call-start = ((), (), s32[]{:S(2)}) async-start(), calls=%async_computation.18 | async-start | bytes 5308416 | tf_op jit(solution)/shard_map/reduce_scatter | solution.py:374
  313.9 5.9 copy-start.11
  323.6 12.1 %copy-start.59 = (s32[8]{0:T(128)S(1)}, s32[8]{0:T(128)}, u32[]{:S(2)}) copy-start(s32[8]{0:T(128)} %dynamic_slice.50) | copy-start | bytes 100
  340.1 654.5 %reduce-scatter.21.cloned.1.call-start = ((), (), s32[]{:S(2)}) async-start(), calls=%async_computation.19 | async-start | bytes 11943936 | tf_op jit(solution)/shard_map/reduce_scatter | solution.py:369
  347.2 14.7 %copy-start.41 = (f32[512]{0:T(512)S(1)}, f32[512]{0:T(512)}, u32[]{:S(2)}) copy-start(f32[512]{0:T(512)} %copy-done.39) | copy-start | bytes 6148
  349.3 16.2 %copy-start.35 = (f32[6,288]{1,0:T(8,128)S(1)}, f32[6,288]{1,0:T(8,128)}, u32[]{:S(2)}) copy-start(f32[6,288]{1,0:T(8,128)} %get-tuple-element.148) | copy-start | bytes 20740
  349.3 16.2 %copy-start.49 = (f32[288]{0:T(512)S(1)}, f32[288]{0:T(512)}, u32[]{:S(2)}) copy-start(f32[288]{0:T(512)} %get-tuple-element.111) | copy-start | bytes 3460
  349.3 16.2 %copy-start.50 = (f32[288]{0:T(512)S(1)}, f32[288]{0:T(512)}, u32[]{:S(2)}) copy-start(f32[288]{0:T(512)} %get-tuple-element.116) | copy-start | bytes 3460
  349.3 16.2 %copy-start.52 = (f32[1152]{0:T(1024)S(1)}, f32[1152]{0:T(1024)}, u32[]{:S(2)}) copy-start(f32[1152]{0:T(1024)} %get-tuple-element.114) | copy-start | bytes 13828
  349.3 58.3 %collective-permute-start.6 = (bf16[128,288]{0,1:T(8,128)(2,1)S(1)}, bf16[128,288]{0,1:T(8,128)(2,1)}, u32[]{:S(2)}, u32[]{:S(2)}) collective-permute-start(bf16[128,288]{0,1:T(8,128)(2,1)S(1)} %slice.213), channel_id=1, source_target_pairs={{4,0},{8,4},{12,8},{16,12},{20,16},{24,20},{28,24},{5,1},{9,5},{13... | collective-permute-start | bytes 221192 | tf_op jit(solution)/shard_map/ppermute | solution.py:19
  361.9 48.0 %copy-start.36 = (s32[1024]{0:T(1024)S(1)}, s32[1024]{0:T(1024)}, u32[]{:S(2)}) copy-start(s32[1024]{0:T(1024)} %get-tuple-element.151) | copy-start | bytes 12292
  364.2 43.5 %collective-permute-start.10 = (bf16[128,288]{0,1:T(8,128)(2,1)S(1)}, bf16[128,288]{0,1:T(8,128)(2,1)S(1)}, u32[]{:S(2)}, u32[]{:S(2)}) collective-permute-start(bf16[128,288]{0,1:T(8,128)(2,1)S(1)} %slice.222), channel_id=1, source_target_pairs={{4,0},{8,4},{12,8},{16,12},{20,16},{24,20},{28,24},{5,1},{9,5},{13... | collective-permute-start | bytes 221192 | tf_op jit(solution)/shard_map/ppermute | solution.py:19
  419.9 574.7 %copy-start.1 = (bf16[1152,1152]{1,0:T(8,128)(2,1)S(1)}, bf16[1152,1152]{1,0:T(8,128)(2,1)}, u32[]{:S(2)}) copy-start(bf16[1152,1152]{1,0:T(8,128)(2,1)} %param.40) | copy-start | bytes 7962628
  (46 other events, 136.0 us)
Sparse Core Ops, SparseCore 0:
  34.9 19.8 all-gather.4
  94.7 28.7 reduce-scatter.10
  126.1 17.4 all-gather.6
  145.2 18.3 all-gather.8
  173.3 25.7 reduce-scatter.14
  201.5 25.7 reduce-scatter.12
  231.2 17.4 all-gather.10
  290.6 26.5 reduce-scatter.16
  321.3 66.2 reduce-scatter.24
  392.0 103.1 reduce-scatter.28
  499.4 103.9 reduce-scatter.26
  607.8 103.7 reduce-scatter.22
  715.8 95.0 reduce-scatter.18
  814.9 179.6 reduce-scatter.20
